TPU v7x, 256 devices: a whole 4x4x8 slice. The times are simulated.
256 devices in a mesh: cells: 16 (over x, y), levels: 16 (over z, core).
Axes of the slice: x: 4, y: 4, z: 8, core: 2. Of those that a mesh axis runs over, the one named last changes fastest.
Arguments:
- populations: float32 [8192, 4096], P('cells', 'levels'), may hold values from 0.05 to 2
- face_speed: float32 [8193], replicated, may hold values from -1 to 1
- cell_class: int32 [8192, 1], P('cells'), may hold values from 0 to 15; in each aligned block of 512 rows (0 to 511, 512 to 1023, ...) at most 64 rows name the same one
- class_offset: bfloat16 [8192], P('cells'), may hold values from -1 to 1
- rate_matrix: bfloat16 [16, 4096, 4096], P('cells', 'levels'), may hold values from -0.09375 to 0.09375
- slope_matrix: bfloat16 [16, 4096, 4096], P('cells', 'levels'), may hold values from -0.09375 to 0.09375
- rate_scale: float32 [16, 4096], P('cells', 'levels'), may hold values from 0.2 to 2
- slope_scale: float32 [16, 4096], P('cells', 'levels'), may hold values from 0.2 to 2
Outputs:
- sources: float32 [8192, 4096], P('cells', 'levels')
- updated: float32 [8192, 4096], P('cells', 'levels')
Inputs may be any that keep to these rules, and one draw needn't show every extreme that they name: `cell_class`: among the cells of one index of the cells axis (aligned blocks of 512 cells) no class is named by more than 64 cells.
All inputs are finite; a program needn't handle non-finite values.
Results may differ from a plain program's by a relative error of at most 0.0029.
Values may be sent and summed in bfloat16 or wider, within the bound.
A program may use at most 64 MiB of HBM per device.

v0:
```python
import jax
import jax.numpy as jnp
from jax import lax
from jax.sharding import PartitionSpec as P

cfl_number = 0.4
step_size = 0.5
spread = 1.25


def padded_2(x, sides, width):
    for axis, dim in sides:
        count, length = (lax.axis_size(axis), x.shape[dim])
        up = [(i, (i + 1) % count) for i in range(count - 1)]
        down = [(j, i) for i, j in up]
        last = lax.slice_in_dim(x, length - width, length, axis=dim)
        first = lax.slice_in_dim(x, 0, width, axis=dim)
        before = lax.ppermute(last, axis, up)
        after = lax.ppermute(first, axis, down)
        x = jnp.concatenate([before, x, after], axis=dim)
    return x


def contract(rows, matrix):
    return lax.dot_general(
        rows, matrix, (((1,), (1,)), ((), ())), preferred_element_type=jnp.float32
    )


def shards(
    populations,
    face_speed,
    cell_class,
    class_offset,
    rate_matrix,
    slope_matrix,
    rate_scale,
    slope_scale,
):
    row_count = populations.shape[0]
    owners = lax.axis_size("cells")
    first_cell = lax.axis_index("cells") * row_count
    speeds = lax.dynamic_slice_in_dim(face_speed, first_cell, row_count + 1)
    padded = padded_2(populations, (("cells", 0),), 1)
    left = padded[:-1]
    right = padded[1:]
    face_flux = 0.5 * speeds[:, None] * (left + right) - 0.5 * spread * (right - left)
    transported = populations + cfl_number * (face_flux[:-1] - face_flux[1:])
    narrow = transported.astype(jnp.bfloat16)
    classes = cell_class[:, 0]
    capacity = 2 * row_count // owners
    one_hot = (classes[:, None] == jnp.arange(owners, dtype=jnp.int32)[None, :]).astype(jnp.int32)
    class_rank = jnp.sum((jnp.cumsum(one_hot, axis=0) - 1) * one_hot, axis=1)
    slot_index = classes * capacity + class_rank
    offsets_sent = (
        jnp.zeros((owners * capacity,), jnp.bfloat16)
        .at[slot_index]
        .set(class_offset)
        .reshape(owners, capacity)
    )
    rate_rows = rate_matrix[0]
    slope_rows = slope_matrix[0]
    rate_gain = rate_scale[0][None, :]
    slope_gain = slope_scale[0][None, :]
    send_rows = (
        jnp.zeros((owners * capacity, narrow.shape[1]), jnp.bfloat16).at[slot_index].set(narrow)
    )
    send_rows = send_rows.reshape(owners, capacity, narrow.shape[1])
    rows = lax.all_to_all(send_rows, "cells", split_axis=0, concat_axis=0, tiled=True)
    offsets = lax.all_to_all(offsets_sent, "cells", split_axis=0, concat_axis=0, tiled=True)
    flat_rows = rows.reshape(-1, rows.shape[2])
    column_block = lax.all_gather(flat_rows, "levels", axis=1, tiled=True)
    rate_part = contract(column_block, rate_rows)
    slope_part = contract(column_block, slope_rows)
    finish_offsets = offsets.reshape(-1)
    values = (
        rate_gain * rate_part
        + slope_gain * finish_offsets.astype(jnp.float32)[:, None] * slope_part
    )
    values = values.reshape(rows.shape[0], rows.shape[1], -1)
    returned = lax.all_to_all(values, "cells", split_axis=0, concat_axis=0, tiled=True)
    sources = returned.reshape(owners * capacity, -1)[slot_index]
    updated = transported + step_size * sources
    return (sources, updated)


def solution(mesh):
    in_specs = (
        P("cells", "levels"),
        P(),
        P("cells", None),
        P("cells"),
        P("cells", "levels", None),
        P("cells", "levels", None),
        P("cells", "levels"),
        P("cells", "levels"),
    )
    out_specs = (P("cells", "levels"), P("cells", "levels"))
    return jax.shard_map(shards, mesh=mesh, in_specs=in_specs, out_specs=out_specs, check_vma=False)
```

profile of v0, /device:TPU:1, one launch (start us, length us, event | category | flops | bytes accessed | tf_op | source)
XLA Modules:
  0.0 151.4 jit_solution(8984078488114040095)
XLA Ops:
  7.2 0.9 fusion.24
  8.1 4.0 %collective-permute-start = (f32[1,256]{1,0:T(1,128)S(1)}, f32[1,256]{1,0:T(1,128)S(1)}, u32[]{:S(2)}, u32[]{:S(2)}) collective-permute-start(f32[1,256]{1,0:T(1,128)S(1)} %get-tuple-element.2), channel_id=1, source_target_pairs={{0,16},{16,32},{32,48},{48,64},{64,80},{80,96},{96,112},{112,128},... | collective-permute-start | bytes 3080 | tf_op jit(solution)/shard_map/ppermute | solution.py:18
  12.2 1.3 collective-permute-start.1
  13.5 1.1 constant_dynamic-update-slice_fusion
  14.5 0.7 fusion.20
  15.2 1.1 reduce-window.6
  16.4 0.2 slice_reduce_fusion
  16.6 0.8 fusion.19
  17.4 0.7 compare_select_fusion
  18.1 0.8 dynamic-slice_multiply_fusion
  18.9 0.8 copy-done.3
  19.7 1.4 multiply_subtract_fusion
  21.1 3.2 %scatter_custom_fusion = bf16[1024,256]{1,0:T(8,128)(2,1)} fusion(s32[512]{0:T(512)S(1)} %bitcast.47, bf16[]{:T(256)} %constant.12.clone.1, f32[512,256]{1,0:T(8,128)S(1)} %copy-done.2, f32[513,256]{1,0:T(8,128)S(1)} %multiply_subtract_fusion), kind=kCustom, calls=%fused_computation.16 | custom fusion | flops 524288 | bytes 2097154 | tf_op jit(solution)/shard_map/scatter | solution.py:66
  24.3 16.6 %all_to_all.20 = bf16[16,64,256]{2,1,0:T(8,128)(2,1)} all-to-all(bf16[16,64,256]{2,1,0:T(8,128)(2,1)} %bitcast.42), channel_id=1, replica_groups=mesh['cells'=16,'levels'=16] {'cells'}, dimensions={0} | all-to-all | bytes 1048576 | tf_op jit(solution)/shard_map/all_to_all | solution.py:69
  41.0 3.9 %scatter_custom_fusion.1 = bf16[1024]{0:T(1024)(128)(2,1)S(1)} fusion(s32[512]{0:T(512)S(1)} %bitcast.48, bf16[512]{0:T(512)(128)(2,1)} %param.11, bf16[]{:T(256)} %constant.12.clone.1), kind=kCustom, calls=%fused_computation.32 | custom fusion | bytes 2560 | tf_op jit(solution)/shard_map/scatter | solution.py:58
  45.0 10.5 %all_to_all.21 = bf16[16,1,64]{2,1,0:T(2,128)(2,1)S(1)} all-to-all(bf16[16,1,64]{2,1,0:T(2,128)(2,1)S(1)} %all_to_all.16), channel_id=1, replica_groups=mesh['cells'=16,'levels'=16] {'cells'}, dimensions={0} | all-to-all | bytes 4096 | tf_op jit(solution)/shard_map/all_to_all | solution.py:70
  55.6 53.2 %all-gather.2.cloned.1.call-done = bf16[1024,4096]{1,0:T(8,128)(2,1)} async-done(((bf16[1024,256]{1,0:T(8,128)(2,1)}), bf16[1024,4096]{1,0:T(8,128)(2,1)}) %all-gather.2.cloned.1.call-update) | async-done | bytes 8388624 | tf_op jit(solution)/shard_map/all_gather | solution.py:72
  108.8 5.9 %fusion.4 = f32[1024,256]{1,0:T(8,128)S(1)} fusion(bf16[1024,4096]{1,0:T(8,128)(2,1)} %all-gather.2.cloned.1.call-done, bf16[1,256,4096]{2,1,0:T(8,128)(2,1)S(1)} %copy-done, f32[256]{0:T(256)S(1)} %bitcast.51), kind=kOutput, calls=%fused_computation.7 | convolution fusion | flops 2147745792 | bytes 11535360 | tf_op jit(solution)/shard_map/dot_general | solution.py:25
  114.7 0.4 copy-done.5
  115.1 3.4 %fusion.10 = f32[1024,256]{1,0:T(8,128)} fusion(f32[1024,256]{1,0:T(8,128)S(1)} %fusion.4, bf16[1024,4096]{1,0:T(8,128)(2,1)S(1)} %copy-done.4, bf16[1,256,4096]{2,1,0:T(8,128)(2,1)S(1)} %copy-done.5, f32[1024]{0:T(1024)S(1)} %reshape.55, f32[256]{0:T(256)S(1)} %bitcast.52), kind=kOutput, calls=%fused_computation.9 | convolution fusion | flops 2148270080 | bytes 12588032 | tf_op jit(solution)/shard_map/dot_general | solution.py:25
  118.5 5.5 %all-to-all-start.2 = ((f32[16,64,256]{2,1,0:T(8,128)}), f32[16,64,256]{2,1,0:T(8,128)S(1)}, u32[]{:S(2)}, u32[]{:S(2)}) async-start(f32[16,64,256]{2,1,0:T(8,128)} %bitcast.44), calls=%async_computation.2 | async-start | bytes 2097152 | tf_op jit(solution)/shard_map/all_to_all | solution.py:81
  124.0 15.8 %all-to-all-done.2 = f32[16,64,256]{2,1,0:T(8,128)S(1)} async-done(((f32[16,64,256]{2,1,0:T(8,128)}), f32[16,64,256]{2,1,0:T(8,128)S(1)}, u32[]{:S(2)}, u32[]{:S(2)}) %all-to-all-start.2) | async-done | bytes 1048608 | tf_op jit(solution)/shard_map/all_to_all | solution.py:81
  139.8 2.2 %gather_fusion = f32[512,256]{1,0:T(8,128)} fusion(f32[1024,256]{1,0:T(8,128)S(1)} %bitcast.41, s32[1024]{0:T(1024)S(1)} %pad_clamp_fusion), kind=kCustom, calls=%fused_computation | custom fusion | bytes 1050624 | tf_op jit(solution)/shard_map/gather | solution.py:82
  142.1 2.5 %multiply_add_fusion = f32[512,256]{1,0:T(8,128)} fusion(f32[512,256]{1,0:T(8,128)} %gather_fusion, f32[512,256]{1,0:T(8,128)} %param.8, f32[513,256]{1,0:T(8,128)} %copy-done.1), kind=kLoop, calls=%fused_computation.15 | loop fusion | flops 655360 | bytes 2621440 | tf_op jit(solution)/shard_map/add | solution.py:83
  (25 shorter events, 0.3 us)
Async XLA Ops:
  7.2 101.6 %copy-start = (bf16[1,256,4096]{2,1,0:T(8,128)(2,1)S(1)}, bf16[1,256,4096]{2,1,0:T(8,128)(2,1)}, u32[]{:S(2)}) copy-start(bf16[1,256,4096]{2,1,0:T(8,128)(2,1)} %param.12) | copy-start | bytes 6291460
  7.2 13.9 %copy-start.2 = (f32[512,256]{1,0:T(8,128)S(1)}, f32[512,256]{1,0:T(8,128)}, u32[]{:S(2)}) copy-start(f32[512,256]{1,0:T(8,128)} %param.8) | copy-start | bytes 1572868
  7.2 101.6 %all-gather.2.cloned.1.call-start = ((), (), s32[]{:S(2)}) async-start(), calls=%async_computation.3 | async-start | bytes 8912896 | tf_op jit(solution)/shard_map/all_gather | solution.py:72
  8.1 11.5 %collective-permute-start = (f32[1,256]{1,0:T(1,128)S(1)}, f32[1,256]{1,0:T(1,128)S(1)}, u32[]{:S(2)}, u32[]{:S(2)}) collective-permute-start(f32[1,256]{1,0:T(1,128)S(1)} %get-tuple-element.2), channel_id=1, source_target_pairs={{0,16},{16,32},{32,48},{48,64},{64,80},{80,96},{96,112},{112,128},... | collective-permute-start | bytes 3080 | tf_op jit(solution)/shard_map/ppermute | solution.py:18
  12.2 6.7 %collective-permute-start.1 = (f32[1,256]{1,0:T(1,128)S(1)}, f32[1,256]{1,0:T(1,128)S(1)}, u32[]{:S(2)}, u32[]{:S(2)}) collective-permute-start(f32[1,256]{1,0:T(1,128)S(1)} %get-tuple-element.3), channel_id=1, source_target_pairs={{16,0},{32,16},{48,32},{64,48},{80,64},{96,80},{112,96},{128,112},... | collective-permute-start | bytes 3080 | tf_op jit(solution)/shard_map/ppermute | solution.py:19
  18.9 0.8 copy-start.3
  21.1 93.6 %copy-start.1 = (f32[513,256]{1,0:T(8,128)}, f32[513,256]{1,0:T(8,128)S(1)}, u32[]{:S(2)}) copy-start(f32[513,256]{1,0:T(8,128)S(1)} %multiply_subtract_fusion) | copy-start | bytes 1575940
  21.1 87.7 %copy-start.6 = (f32[1,256]{1,0:T(1,128)S(1)}, f32[1,256]{1,0:T(1,128)}, u32[]{:S(2)}) copy-start(f32[1,256]{1,0:T(1,128)} %param.14) | copy-start | bytes 3076
  108.7 5.9 %copy-start.4 = (bf16[1024,4096]{1,0:T(8,128)(2,1)S(1)}, bf16[1024,4096]{1,0:T(8,128)(2,1)}, u32[]{:S(2)}) copy-start(bf16[1024,4096]{1,0:T(8,128)(2,1)} %all-gather.2.cloned.1.call-done) | copy-start | bytes 25165828
  108.7 6.4 %copy-start.5 = (bf16[1,256,4096]{2,1,0:T(8,128)(2,1)S(1)}, bf16[1,256,4096]{2,1,0:T(8,128)(2,1)}, u32[]{:S(2)}) copy-start(bf16[1,256,4096]{2,1,0:T(8,128)(2,1)} %param.13) | copy-start | bytes 6291460
  108.8 6.4 %copy-start.7 = (f32[1,256]{1,0:T(1,128)S(1)}, f32[1,256]{1,0:T(1,128)}, u32[]{:S(2)}) copy-start(f32[1,256]{1,0:T(1,128)} %param.15) | copy-start | bytes 3076
  118.5 21.4 %all-to-all-start.2 = ((f32[16,64,256]{2,1,0:T(8,128)}), f32[16,64,256]{2,1,0:T(8,128)S(1)}, u32[]{:S(2)}, u32[]{:S(2)}) async-start(f32[16,64,256]{2,1,0:T(8,128)} %bitcast.44), calls=%async_computation.2 | async-start | bytes 2097152 | tf_op jit(solution)/shard_map/all_to_all | solution.py:81
Sparse Core Ops, SparseCore 0:
  41.1 67.6 all-gather.1
where the time goes:
time: 153 us; the launch traced here: 151 us
  waiting for transfers between devices  69 us (45%)
  blocking collectives  27.1 us (18%)
  between operations  14.2 us (9%)
  other arithmetic  11.2 us (7%)
  starting transfers between devices  10.9 us (7%)
  local copies, waits for them, and re-layouts  9.76 us (6%)
  matrix products  9.27 us (6%)
    all_gather x1, waiting for transfers between devices, shards(): column_block = lax.all_gather(flat_rows, 'levels', axis=1, tiled=True)  53.2 us
    all_to_all x1, blocking collectives, shards(): lax.all_to_all(send_rows, 'cells', split_axis=0, concat_axis=0, tiled=True)  16.6 us
    all_to_all x1, waiting for transfers between devices, shards(): lax.all_to_all(values, 'cells', split_axis=0, concat_axis=0, tiled=True)  15.8 us
    all_to_all x1, blocking collectives, shards(): lax.all_to_all(offsets_sent, 'cells', split_axis=0, concat_axis=0, tiled=...  10.5 us
    dot_general x2, matrix products, contract(): lax.dot_general(rows, matrix, (((1,), (1,)), ((), ())), preferred_element...  9.27 us
    all_to_all x1, starting transfers between devices, shards(): lax.all_to_all(values, 'cells', split_axis=0, concat_axis=0, tiled=True)  5.54 us
    ppermute x1, starting transfers between devices, padded_2(): before = lax.ppermute(last, axis, up)  4.01 us
    scatter x1, local copies, waits for them, and re-layouts, shards(): offsets_sent = jnp.zeros((owners * capacity,), jnp.bfloat16).at[slot_inde...  3.92 us
  transfers between devices with their start and end apart: 4, of which 2 were waited for; matrix products, arithmetic and copies ran while one was open for 6% of the time, Pallas kernels for 0%

commit v1 on v0

v1 whole, which is shorter than its diff:
```python
import functools

import jax
import jax.numpy as jnp
from jax import lax
from jax.experimental import pallas as pl
from jax.experimental.pallas import tpu as pltpu
from jax.sharding import PartitionSpec as P

MESH = pl.DeviceIdType.MESH
F32 = jnp.float32
BF16 = jnp.bfloat16
I32 = jnp.int32

SIDE = 4
RING = 8
LAG = 2


def iota(shape, dim):
    return lax.broadcasted_iota(I32, shape, dim)


def remote(src, dst, send, recv, device):
    return pltpu.make_async_remote_copy(
        src_ref=src, dst_ref=dst, send_sem=send, recv_sem=recv, device_id=device, device_id_type=MESH
    )


def nt(a, b):
    return lax.dot_general(a, b, (((1,), (1,)), ((), ())), preferred_element_type=F32)


def kernel(
    small, pop, rate, slope, rate_gain, slope_gain, sources, updated,
    pad, wr, ws, x, send, off_send, off_recv, back_send, back, pick, moved,
    local_sem, halo_send, halo_recv, out_send, row_recv, offs_recv, ring_recv, pair_recv, back_recv,
):
    rows, width = sources.shape
    groups = SIDE * SIDE
    cap = send.shape[0] // groups
    c = lax.axis_index("cells")
    lev = lax.axis_index("levels")
    cx, cy = lax.div(c, SIDE), lax.rem(c, SIDE)
    z, h = lax.div(lev, 2), lax.rem(lev, 2)
    other = 1 - h
    right = lax.rem(z + 1, RING) * 2 + h
    left = lax.rem(z + RING - 1, RING) * 2 + h
    twin = z * 2 + other
    cell_up = lax.rem(c + 1, groups)
    cell_down = lax.rem(c + groups - 1, groups)

    pop_copy = pltpu.make_async_copy(pop, pad.at[pl.ds(8, rows)], local_sem.at[0])
    rate_copy = pltpu.make_async_copy(rate.at[0], wr, local_sem.at[1])
    slope_copy = pltpu.make_async_copy(slope.at[0], ws, local_sem.at[2])
    pop_copy.start()
    rate_copy.start()
    slope_copy.start()

    def toward(g):
        return lax.rem(cx + SIDE - g // SIDE, SIDE) * SIDE + lax.rem(cy + SIDE - g % SIDE, SIDE)

    def origin(g):
        return lax.rem(cx + lax.div(g, SIDE), SIDE) * SIDE + lax.rem(cy + lax.rem(g, SIDE), SIDE)

    barrier = pltpu.get_barrier_semaphore()
    for g in range(1, groups):
        pl.semaphore_signal(barrier, inc=1, device_id=(toward(g), lev), device_id_type=MESH)
    for peer in (right, left, twin):
        pl.semaphore_signal(barrier, inc=1, device_id=(c, peer), device_id_type=MESH)

    quarter = rows // 4
    cls = jnp.concatenate([small[pl.ds(8 + q, 1), :] for q in range(4)], axis=1).astype(I32)
    hot = (iota((groups, rows), 0) == cls).astype(F32)
    earlier = (iota((rows, rows), 0) < iota((rows, rows), 1)).astype(F32).astype(BF16)
    before = jnp.dot(hot.astype(BF16), earlier, preferred_element_type=F32)
    rank = jnp.sum(hot * before, axis=0, keepdims=True).astype(I32)
    gx = (cx - (cls >> 2)) & (SIDE - 1)
    gy = (cy - (cls & (SIDE - 1))) & (SIDE - 1)
    slot = (gx * SIDE + gy) * cap + rank

    slot4 = jnp.concatenate([slot[:, q * quarter : (q + 1) * quarter] for q in range(4)], axis=0)
    columns = jnp.concatenate([small[...], slot4.astype(F32), jnp.zeros((108, 128), F32)], axis=0).T

    def column(i):
        return columns[:, i : i + 1]

    pop_copy.wait()
    pl.semaphore_wait(barrier, groups - 1 + 3)

    up = remote(
        pad.at[pl.ds(rows, 8)], pad.at[pl.ds(0, 8)], halo_send.at[0], halo_recv.at[0], (cell_up, lev)
    )
    down = remote(
        pad.at[pl.ds(8, 8)], pad.at[pl.ds(rows + 8, 8)], halo_send.at[1], halo_recv.at[1], (cell_down, lev)
    )
    up.start()
    down.start()

    for q in range(4):
        pick[pl.ds(q * quarter, quarter), :] = (
            (iota((quarter, groups * cap), 1) == column(16 + q).astype(I32)).astype(F32).astype(BF16)
        )
    offsets = jnp.concatenate(
        [jnp.broadcast_to(column(12 + q), (quarter, 128)) for q in range(4)], axis=0
    ).astype(BF16)

    up.wait()
    down.wait()

    @pl.when(c == 0)
    def _():
        pad[pl.ds(0, 8), :] = jnp.zeros((8, width), F32)

    @pl.when(c == groups - 1)
    def _():
        pad[pl.ds(rows + 8, 8), :] = jnp.zeros((8, width), F32)

    narrow = []
    for q in range(4):
        a = pad[pl.ds(q * quarter + 7, quarter), :]
        b = pad[pl.ds(q * quarter + 8, quarter), :]
        d = pad[pl.ds(q * quarter + 9, quarter), :]
        lower = 0.5 * column(q) * (a + b) - 0.625 * (b - a)
        upper = 0.5 * column(4 + q) * (b + d) - 0.625 * (d - b)
        t = b + 0.4 * (lower - upper)
        moved[pl.ds(q * quarter, quarter), :] = t
        narrow.append(t.astype(BF16))
    table = jnp.concatenate([jnp.concatenate(narrow, axis=0), offsets], axis=1)

    def rows_of(g):
        return pl.ds(pl.multiple_of(g * cap, cap), cap)

    def row_copy(g, device):
        return remote(
            send.at[rows_of(g)], x.at[h, z, rows_of(g)], out_send.at[0], row_recv.at[g], device
        )

    def off_copy(g, device):
        return remote(
            off_send.at[rows_of(g)], off_recv.at[rows_of(g)], out_send.at[1], offs_recv.at[g], device
        )

    for q in range(4):
        take = (iota((4 * cap, rows), 0) + 4 * cap * q == slot).astype(F32).astype(BF16)
        routed = jnp.dot(take, table, preferred_element_type=F32).astype(BF16)
        if q == 0:
            x[h, z, pl.ds(0, cap), :] = routed[:cap, :width]
            off_recv[pl.ds(0, cap), :] = routed[:cap, width:]
        send[pl.ds(4 * cap * q, 4 * cap), :] = routed[:, :width]
        off_send[pl.ds(4 * cap * q, 4 * cap), :] = routed[:, width:]
        for g in range(max(1, 4 * q), 4 * q + 4):
            row_copy(g, (toward(g), lev)).start()
            off_copy(g, (toward(g), lev)).start()

    rate_copy.wait()
    slope_copy.wait()

    half = cap // 2
    hops = RING // 2

    def ring_copy(g, j, way, device):
        place = lax.rem(z + RING - j, RING) if way == 0 else lax.rem(z + j, RING)
        if j < hops:
            span = rows_of(g)
        else:
            span = pl.ds(pl.multiple_of(g * cap + way * half, half), half)
        return place, span, ring_recv.at[g, way * hops + j - 1], device

    def wait_ring(g, j, way):
        place, span, recv, _ = ring_copy(g, j, way, None)
        ref = x.at[h, place, span]
        remote(ref, ref, out_send.at[2], recv, (c, right)).wait_recv()

    def send_ring(g, j, way):
        if j < hops:
            span = rows_of(g)
        else:
            span = pl.ds(pl.multiple_of(g * cap + way * half, half), half)
        place = lax.rem(z + RING - (j - 1), RING) if way == 0 else lax.rem(z + j - 1, RING)
        ref = x.at[h, place, span]
        remote(
            ref, ref, out_send.at[3 + way * hops + j - 1], ring_recv.at[g, way * hops + j - 1],
            (c, right if way == 0 else left),
        ).start()

    def send_twin(g, place):
        ref = x.at[h, place, rows_of(g)]
        remote(ref, ref, out_send.at[2], pair_recv.at[g], (c, twin)).start()

    def back_copy(g, device):
        return remote(
            back_send.at[rows_of(g)], back.at[rows_of(g)], out_send.at[11], back_recv.at[g], device
        )

    pair = 2 * cap

    def tick(t, carry):
        for j in range(hops, 0, -1):
            g = t - LAG * j

            @pl.when((g >= 0) & (g < groups))
            def _(g=g, j=j):
                for way in range(2):
                    wait_ring(g, j, way)
                    if j < hops:
                        send_ring(g, j + 1, way)
                        send_twin(g, lax.rem(z + RING - j, RING) if way == 0 else lax.rem(z + j, RING))
                if j == hops:
                    send_twin(g, lax.rem(z + hops, RING))

        @pl.when(t < groups)
        def _():
            @pl.when(t > 0)
            def _():
                row_copy(t, (c, lev)).wait_recv()

            for way in range(2):
                send_ring(t, 1, way)
            send_twin(t, z)

        g = t - LAG * (hops + 1)

        @pl.when((g >= 0) & (lax.rem(g + 2, 2) == 1))
        def _():
            for i in range(2):
                span = rows_of(g - 1 + i)
                ref = x.at[other, :, span]
                pltpu.make_async_copy(ref, ref, pair_recv.at[g - 1 + i]).wait()

            @pl.when(g > 1)
            def _():
                off_copy(g - 1, (c, lev)).wait_recv()

            off_copy(g, (c, lev)).wait_recv()
            both = pl.ds(pl.multiple_of((g - 1) * cap, pair), pair)
            rate_part = jnp.zeros((pair, width), F32)
            slope_part = jnp.zeros((pair, width), F32)
            for i in range(2 * RING):
                chunk = x[i // RING, i % RING, both, :]
                lanes = pl.ds((2 * (i % RING) + i // RING) * width, width)
                rate_part += nt(chunk, wr[:, lanes])
                slope_part += nt(chunk, ws[:, lanes])
            o = off_recv[both, :].astype(F32)
            o = jnp.concatenate([o] * (width // 128), axis=1)
            values = rate_gain[...] * rate_part + slope_gain[...] * o * slope_part
            back_send[both, :] = values.astype(BF16)

            @pl.when(g == 1)
            def _():
                back[pl.ds(0, cap), :] = values[:cap].astype(BF16)

            @pl.when(g > 1)
            def _():
                back_copy(g - 1, (origin(g - 1), lev)).start()

            back_copy(g, (origin(g), lev)).start()

        return carry

    lax.fori_loop(0, groups + LAG * (hops + 1), tick, 0)

    total = jnp.zeros((rows, width), F32)
    for q in range(4):
        for g in range(max(1, 4 * q), 4 * q + 4):
            back_copy(g, (c, lev)).wait_recv()
        span = pl.ds(4 * cap * q, 4 * cap)
        total += jnp.dot(pick[:, span], back[span, :], preferred_element_type=F32)
    sources[...] = total
    updated[...] = moved[...] + 0.5 * total

    def drain(ref, sem):
        pltpu.make_async_copy(ref, ref, sem).wait()

    rest = pl.ds(cap, (groups - 1) * cap)
    drain(send.at[rest], out_send.at[0])
    drain(off_send.at[rest], out_send.at[1])
    drain(x.at[0], out_send.at[2])
    for way in range(2):
        for j in range(1, hops):
            drain(x.at[0, 0], out_send.at[3 + way * hops + j - 1])
        drain(x.at[0, 0, pl.ds(0, groups * half)], out_send.at[3 + way * hops + hops - 1])
    drain(back_send.at[rest], out_send.at[11])


def shards(
    populations, face_speed, cell_class, class_offset, rate_matrix, slope_matrix, rate_scale, slope_scale
):
    rows, width = populations.shape
    groups = SIDE * SIDE
    cap = 2 * rows // groups
    slots = groups * cap
    first = lax.axis_index("cells") * rows
    speeds = lax.dynamic_slice_in_dim(face_speed, first, rows + 1)
    small = jnp.concatenate(
        [
            speeds[:-1].reshape(4, -1),
            speeds[1:].reshape(4, -1),
            cell_class.reshape(4, -1).astype(F32),
            class_offset.astype(F32).reshape(4, -1),
        ],
        axis=0,
    )
    vmem = pl.BlockSpec(memory_space=pltpu.VMEM)
    hbm = pl.BlockSpec(memory_space=pl.ANY)
    out = jax.ShapeDtypeStruct((rows, width), F32)
    dma = pltpu.SemaphoreType.DMA
    return pl.pallas_call(
        kernel,
        out_shape=(out, out),
        in_specs=[vmem, hbm, hbm, hbm, vmem, vmem],
        out_specs=(vmem, vmem),
        scratch_shapes=[
            pltpu.VMEM((rows + 16, width), F32),
            pltpu.VMEM(rate_matrix.shape[1:], BF16),
            pltpu.VMEM(slope_matrix.shape[1:], BF16),
            pltpu.VMEM((2, RING, slots, width), BF16),
            pltpu.VMEM((slots, width), BF16),
            pltpu.VMEM((slots, 128), BF16),
            pltpu.VMEM((slots, 128), BF16),
            pltpu.VMEM((slots, width), BF16),
            pltpu.VMEM((slots, width), BF16),
            pltpu.VMEM((rows, slots), BF16),
            pltpu.VMEM((rows, width), F32),
            dma((3,)),
            dma((2,)),
            dma((2,)),
            dma((12,)),
            dma((groups,)),
            dma((groups,)),
            dma((groups, RING)),
            dma((groups,)),
            dma((groups,)),
        ],
        compiler_params=pltpu.CompilerParams(
            collective_id=0, has_side_effects=True, vmem_limit_bytes=60 * 1024 * 1024
        ),
    )(small, populations, rate_matrix, slope_matrix, rate_scale, slope_scale)


def solution(mesh):
    in_specs = (
        P("cells", "levels"),
        P(),
        P("cells", None),
        P("cells"),
        P("cells", "levels", None),
        P("cells", "levels", None),
        P("cells", "levels"),
        P("cells", "levels"),
    )
    out_specs = (P("cells", "levels"), P("cells", "levels"))
    return jax.shard_map(shards, mesh=mesh, in_specs=in_specs, out_specs=out_specs, check_vma=False)
```

time: 153 us -> 85.9 us (0.56)
  the two profiles are of different devices: /device:TPU:1 before, /device:TPU:14 now
where the time goes in v1:
time: 85.9 us; the launch traced here: 85.6 us
  Pallas kernels  78.4 us (91%)
  local copies, waits for them, and re-layouts  4.58 us (5%)
  other arithmetic  1.97 us (2%)
    pallas_call x1, Pallas kernels, shards(): pl.pallas_call(kernel, out_shape=(out, out), in_specs=[vmem, hbm, hbm, hb...  78.4 us
    unnamed x2, local copies, waits for them, and re-layouts  3.74 us

profile of v1, /device:TPU:14, one launch (start us, length us, event | category | flops | bytes accessed | tf_op | source)
XLA Modules:
  0.0 85.6 jit_solution(1483071323483229339)
XLA Ops:
  0.6 0.7 convert_element_type.7
  1.3 0.7 bitcast_convert_fusion
  2.0 0.8 dynamic_slice.3
  2.8 0.1 slice_bitcast_fusion.1
  2.8 0.6 pad_maximum_fusion.small
  3.5 78.4 %shard_map.95 = (f32[512,256]{1,0:T(8,128)}, f32[512,256]{1,0:T(8,128)}) custom-call(f32[16,128]{1,0:T(8,128)} %pad_maximum_fusion.small, f32[512,256]{1,0:T(8,128)} %pop.1, bf16[1,256,4096]{2,1,0:T(8,128)(2,1)} %rate.1, bf16[1,256,4096]{2,1,0:T(8,128)(2,1)} %slope.1, f32[1,256]{1,0:T(1,128)} %rate_gain.1, f32[1,256]{1,0:T(1,128)} %slope_gain.1), custom_call_target="tpu_custom_call" | custom-call | tf_op jit(solution)/shard_map/pallas_call | solution.py:308
  81.8 1.9 %copy.12 = f32[512,256]{1,0:T(8,128)} copy(f32[512,256]{1,0:T(8,128)} %get-tuple-element.6) | data formatting | bytes 1048576
  83.7 1.9 %copy.13 = f32[512,256]{1,0:T(8,128)} copy(f32[512,256]{1,0:T(8,128)} %get-tuple-element.7) | data formatting | bytes 1048576

commit v2 on v1

v2 whole, which is shorter than its diff:
```python
import jax
import jax.numpy as jnp
from jax import lax
from jax.experimental import pallas as pl
from jax.experimental.pallas import tpu as pltpu
from jax.sharding import PartitionSpec as P

MESH = pl.DeviceIdType.MESH
F32 = jnp.float32
BF16 = jnp.bfloat16
I32 = jnp.int32

SIDE = 4
RING = 8
HOPS = RING // 2


def iota(shape, dim):
    return lax.broadcasted_iota(I32, shape, dim)


def remote(src, dst, send, recv, device):
    return pltpu.make_async_remote_copy(
        src_ref=src, dst_ref=dst, send_sem=send, recv_sem=recv, device_id=device, device_id_type=MESH
    )


def nt(a, b):
    return lax.dot_general(a, b, (((1,), (1,)), ((), ())), preferred_element_type=F32)


def steps_of(g):
    i, j = g // SIDE, g % SIDE
    j = j + (i // 2) * (SIDE - 1 - 2 * j)
    return (i % 2) * 2 + i // 2, j + j // 2 - 2 * (j // 3)


def kernel(
    cls4, off4, speeds, pop, rate, slope, rate_gain, slope_gain, sources, transported,
    pad, wr, ws, x, flat, send, off_send, off_recv, back_send, back, take, pick, moved, acc, result,
    local_sem, halo_send, halo_recv, out_send, row_recv, many_recv, offs_recv, ring_recv, flat_recv,
    padded_twin, flat_twin, back_recv,
):
    rows, width = result.shape
    groups = SIDE * SIDE
    cap = back.shape[0] // groups
    batch = groups // 2
    quarter = rows // 4
    c = lax.axis_index("cells")
    lev = lax.axis_index("levels")
    cx, cy = lax.div(c, SIDE), lax.rem(c, SIDE)
    z, h = lax.div(lev, 2), lax.rem(lev, 2)
    right = lax.rem(z + 1, RING) * 2 + h
    left = lax.rem(z + RING - 1, RING) * 2 + h
    twin = z * 2 + 1 - h
    cell_up = lax.rem(c + 1, groups)
    cell_down = lax.rem(c + groups - 1, groups)

    barrier = pltpu.get_barrier_semaphore()

    def toward(g):
        dx, dy = steps_of(g)
        return lax.rem(cx + SIDE - dx, SIDE) * SIDE + lax.rem(cy + SIDE - dy, SIDE)

    def origin(g):
        i, j = lax.div(g, SIDE), lax.rem(g, SIDE)
        j = j + lax.div(i, 2) * (SIDE - 1 - 2 * j)
        dx = lax.rem(i, 2) * 2 + lax.div(i, 2)
        dy = j + lax.div(j, 2) - 2 * lax.div(j, 3)
        return lax.rem(cx + dx, SIDE) * SIDE + lax.rem(cy + dy, SIDE)

    for g in range(1, groups):
        pl.semaphore_signal(barrier, inc=1, device_id=(toward(g), lev), device_id_type=MESH)
    for peer in (right, left, twin):
        pl.semaphore_signal(barrier, inc=1, device_id=(c, peer), device_id_type=MESH)

    pop_copy = pltpu.make_async_copy(pop, pad.at[pl.ds(8, rows)], local_sem.at[0])
    pop_copy.start()
    for i in range(2 * RING):
        lanes = pl.ds(i * width, width)
        pltpu.make_async_copy(rate.at[0, :, lanes], wr.at[i], local_sem.at[1]).start()
        pltpu.make_async_copy(slope.at[0, :, lanes], ws.at[i], local_sem.at[2]).start()

    cls = jnp.concatenate([cls4[pl.ds(q, 1), :] for q in range(4)], axis=1)
    hot = (iota((groups, rows), 0) == cls).astype(F32)
    earlier = (iota((rows, rows), 0) < iota((rows, rows), 1)).astype(F32).astype(BF16)
    before = jnp.dot(hot.astype(BF16), earlier, preferred_element_type=F32)
    rank = jnp.sum(hot * before, axis=0, keepdims=True).astype(I32)
    dx = (cx - (cls >> 2)) & (SIDE - 1)
    dy = (cy - (cls & (SIDE - 1))) & (SIDE - 1)
    i, j = (dx & 1) * 2 + (dx >> 1), dy ^ (dy >> 1)
    j = j + (i >> 1) * (SIDE - 1 - 2 * j)
    slot = (i * SIDE + j) * cap + rank

    slot4 = jnp.concatenate([slot[:, q * quarter : (q + 1) * quarter] for q in range(4)], axis=0)
    base = pl.multiple_of(c * rows, rows)
    line = [speeds[pl.ds(base + q * quarter, quarter)].reshape(1, quarter) for q in range(4)]
    end = speeds[pl.ds(base + rows, 1)].reshape(1, 1)
    line = jnp.concatenate(line + [jnp.broadcast_to(end, (1, quarter))], axis=1)
    ahead = pltpu.roll(line, 5 * quarter - 1, 1)
    o4 = off4[...].astype(F32).reshape(4, quarter)
    columns = jnp.concatenate(
        [line[:, q * quarter : (q + 1) * quarter] for q in range(4)] +
        [ahead[:, q * quarter : (q + 1) * quarter] for q in range(4)] +
        [slot4.astype(F32), jnp.zeros((116, 128), F32)], axis=0
    ).T

    def column(i):
        return columns[:, i : i + 1]

    pop_copy.wait()
    pl.semaphore_wait(barrier, groups - 1 + 3)

    up = remote(
        pad.at[pl.ds(rows, 8)], pad.at[pl.ds(0, 8)], halo_send.at[0], halo_recv.at[0], (cell_up, lev)
    )
    down = remote(
        pad.at[pl.ds(8, 8)], pad.at[pl.ds(rows + 8, 8)], halo_send.at[1], halo_recv.at[1], (cell_down, lev)
    )
    up.start()
    down.start()

    for q in range(4):
        take[pl.ds(4 * cap * q, 4 * cap), :] = (
            (iota((4 * cap, rows), 0) + 4 * cap * q == slot).astype(F32).astype(BF16)
        )

    up.wait()
    down.wait()

    @pl.when(c == 0)
    def _():
        pad[pl.ds(0, 8), :] = jnp.zeros((8, width), F32)

    @pl.when(c == groups - 1)
    def _():
        pad[pl.ds(rows + 8, 8), :] = jnp.zeros((8, width), F32)

    for q in range(4):
        a = pad[pl.ds(q * quarter + 7, quarter), :]
        b = pad[pl.ds(q * quarter + 8, quarter), :]
        d = pad[pl.ds(q * quarter + 9, quarter), :]
        lower = 0.5 * column(q) * (a + b) - 0.625 * (b - a)
        upper = 0.5 * column(4 + q) * (b + d) - 0.625 * (d - b)
        t = b + 0.4 * (lower - upper)
        moved[pl.ds(q * quarter, quarter), :] = t
        flat[z, pl.ds(q * quarter, quarter), :] = t.astype(BF16)

    offsets = jnp.broadcast_to(
        jnp.concatenate([o4[q : q + 1] for q in range(4)], axis=1), (16, rows)
    ).astype(BF16)
    moved_copy = pltpu.make_async_copy(moved, transported, local_sem.at[0])

    half = cap // 2
    near = batch // 2
    pieces = 4
    piece = rows // pieces
    offset = (0, -1, 1, -2, 2, -3, 3, HOPS)

    def rows_of(g):
        return pl.ds(pl.multiple_of(g * cap, cap), cap)

    def place_at(i):
        return lax.rem(z + RING + i, RING)

    def place_of(j, way):
        return place_at(-j if way == 0 else j)

    def toward_way(way):
        return (c, right if way == 0 else left)

    def each(lower, upper, f):
        def body(g, carry):
            f(g)
            return carry

        lax.fori_loop(lower, upper, body, 0)

    def route(place, b, own_role):
        for q in range(2):
            span = pl.ds((b * batch + q * near) * cap, near * cap)
            got = jnp.dot(take[span, :], flat[place], preferred_element_type=F32).astype(BF16)
            send[place, span, :] = got
            if b == 0 and q == 0:
                x[own_role, place, pl.ds(0, cap), :] = got[:cap]

    def off_copy(g, device):
        return remote(off_send.at[g // 2], off_recv.at[g], out_send.at[1], offs_recv.at[g], device)

    def send_offsets():
        got = nt(offsets, take[...]).astype(BF16)
        for p in range(batch):
            off_send[p] = got[:, 2 * cap * p : 2 * cap * (p + 1)]
        off_recv[0] = got[:, : 2 * cap]
        for g in range(1, groups):
            off_copy(g, (toward(g), lev)).start()

    def make_pick():
        for q in range(4):
            pick[pl.ds(q * quarter, quarter), :] = (
                (iota((quarter, groups * cap), 1) == column(8 + q).astype(I32)).astype(F32).astype(BF16)
            )

    def wait_bytes(ref, sem):
        pltpu.make_async_copy(ref, ref, sem).wait()

    def wait_weights():
        wait_bytes(wr, local_sem.at[1])
        wait_bytes(ws, local_sem.at[2])

    def multiply(b, role, shift, start=0, count=batch, fresh=False):
        place = place_at(shift)
        level = place * 2 + role
        span = pl.ds((b * batch + start) * cap, count * cap)
        chunk = x[role, place, span, :]
        for n, w in ((0, wr), (1, ws)):
            part = nt(chunk, w[level])
            acc[n, span, :] = part if fresh else acc[n, span, :] + part

    def multiply_two(b, role, j):
        each(0, 2, lambda i: multiply(b, role, j * (2 * i - 1)))

    def when(i, at, f):
        pl.when(i == at)(f)

    def back_copy(g, device):
        return remote(
            back_send.at[rows_of(g)], back.at[rows_of(g)], out_send.at[3], back_recv.at[g], device
        )

    def finish(b, start, count):
        base = b * batch + start
        for g in range(max(1, base), base + count):
            off_copy(g, (c, lev)).wait_recv()
        low = iota((1, 2 * cap), 1) < cap
        o = [
            jnp.where(low, off_recv[g, 0:1, :].astype(F32), off_recv[g + 1, 0:1, :].astype(F32))
            for g in range(base, base + count, 2)
        ]
        o = jnp.concatenate(o + [jnp.zeros((128 - len(o), 2 * cap), F32)], axis=0).T
        for p in range(count // 2):
            two = pl.ds((base + 2 * p) * cap, 2 * cap)
            values = rate_gain[...] * acc[0, two, :] + slope_gain[...] * o[:, p : p + 1] * acc[1, two, :]
            back_send[two, :] = values.astype(BF16)
            if base + p == 0:
                back[pl.ds(0, cap), :] = values[:cap].astype(BF16)
        for g in range(max(1, base), base + count):
            back_copy(g, (origin(g), lev)).start()

    def collect(base, count):
        for g in range(max(1, base), base + count):
            back_copy(g, (c, lev)).wait_recv()
        span = pl.ds(base * cap, count * cap)
        return jnp.dot(pick[:, span], back[span, :], preferred_element_type=F32)

    def wait_padded(number, chunks, start, count):
        wait_bytes(x.at[0, pl.ds(0, chunks), pl.ds(start * cap, count * cap)], padded_twin.at[number])

    def wait_flat(number, count=batch):
        wait_bytes(x.at[1, 0, pl.ds(0, count * cap)], flat_twin.at[number])

    @pl.when(h == 0)
    def _():
        def row_copy(g, device):
            return remote(
                send.at[z, rows_of(g)], x.at[0, z, rows_of(g)], out_send.at[0], row_recv.at[g], device
            )

        def span_of(g, j, way):
            if j < HOPS:
                return rows_of(g)
            return pl.ds(pl.multiple_of(g * cap + way * half, half), half)

        def ring_ref(g, j, way, place):
            return x.at[0, place, span_of(g, j, way)]

        def wait_ring(g, j, way):
            ref = ring_ref(g, j, way, place_of(j, way))
            recv = ring_recv.at[g, way * HOPS + j - 1]
            remote(ref, ref, out_send.at[2], recv, toward_way(way)).wait_recv()

        def send_ring(g, j, way):
            ref = ring_ref(g, j, way, place_of(j - 1, way))
            recv = ring_recv.at[g, way * HOPS + j - 1]
            remote(ref, ref, out_send.at[4 if j < HOPS else 5], recv, toward_way(way)).start()

        def send_twin(g, place, number):
            ref = x.at[0, place, rows_of(g)]
            remote(ref, ref, out_send.at[2], padded_twin.at[number], (c, twin)).start()

        def first(g, b):
            if not isinstance(g, int):
                row_copy(g, (c, lev)).wait_recv()

            for way in range(2):
                send_ring(g, 1, way)
            send_twin(g, z, 5 * b)

        def middle(g, b, j):
            for way in range(2):
                wait_ring(g, j, way)
                send_ring(g, j + 1, way)
                send_twin(g, place_of(j, way), 5 * b + j)

        def last(g, number):
            for way in range(2):
                wait_ring(g, HOPS, way)
            send_twin(g, place_of(HOPS, 0), number)

        def send_rows(b):
            route(z, b, 0)
            for g in range(max(1, b * batch), (b + 1) * batch):
                row_copy(g, (toward(g), lev)).start()

        send_rows(0)
        first(0, 0)
        make_pick()
        moved_copy.start()
        each(1, near, lambda g: first(g, 0))

        def start_up(g):
            first(g + near, 0)
            middle(g, 0, 1)

        each(0, near, start_up)
        send_rows(1)
        send_offsets()
        each(near, batch, lambda g: middle(g, 0, 1))
        wait_weights()
        multiply(0, 0, 0, fresh=True)

        def turn_2(i):
            middle(i, 0, 2)
            when(i, 1, lambda: multiply(0, 0, -1))
            when(i, 3, lambda: multiply(0, 0, 1))

        each(0, batch, turn_2)

        def turn_3(i):
            middle(i, 0, 3)
            when(i, 1, lambda: multiply(0, 0, -2))
            when(i, 3, lambda: multiply(0, 0, 2))

            @pl.when(i == 5)
            def _():
                wait_flat(0)
                multiply(0, 1, 0)

        each(0, batch, turn_3)
        each(batch, groups, lambda g: first(g, 1))

        def turn_last(i):
            last(i, HOPS)
            when(i, 1, lambda: multiply(0, 0, -3))
            when(i, 2, lambda: multiply(0, 0, 3))

            @pl.when(i == 4)
            def _():
                wait_flat(1)
                multiply(0, 1, -1)

            @pl.when(i == 6)
            def _():
                wait_flat(2)
                multiply(0, 1, 1)

        each(0, batch, turn_last)

        def turn_over(i):
            middle(batch + i, 1, 1)
            when(i, 0, lambda: multiply(0, 0, HOPS))

            @pl.when(i == 2)
            def _():
                wait_flat(3)
                multiply(0, 1, -2)

            @pl.when(i == 4)
            def _():
                wait_flat(4)
                multiply(0, 1, 2)

            when(i, 6, lambda: multiply(1, 0, 0, fresh=True))

        each(0, batch, turn_over)

        def turn_6(i):
            middle(batch + i, 1, 2)

            @pl.when(i == 0)
            def _():
                wait_flat(5)
                multiply(0, 1, -3)

            @pl.when(i == 2)
            def _():
                wait_flat(6)
                multiply(0, 1, 3)

            @pl.when(i == 4)
            def _():
                wait_flat(7)
                multiply(0, 1, HOPS)
                finish(0, 0, batch)

            when(i, 5, lambda: multiply(1, 0, -1))
            when(i, 6, lambda: multiply(1, 0, 1))

        each(0, batch, turn_6)

        def turn_7(i):
            middle(batch + i, 1, 3)

            @pl.when(i == 0)
            def _():
                wait_flat(8)
                multiply(1, 1, 0)

            when(i, 1, lambda: multiply(1, 0, -2))
            when(i, 2, lambda: multiply(1, 0, 2))

            @pl.when(i == 4)
            def _():
                wait_flat(9)
                multiply(1, 1, -1)

            @pl.when(i == 6)
            def _():
                wait_flat(10)
                multiply(1, 1, 1)

        each(0, batch, turn_7)
        each(0, 2, lambda i: multiply(1, 0, 3 * (2 * i - 1)))
        each(batch, batch + near, lambda g: last(g, 5 + HOPS))
        each(batch + near, groups, lambda g: last(g, 5 + HOPS + 1))
        multiply(1, 0, HOPS)
        wait_flat(11)
        multiply(1, 1, -2)
        wait_flat(12)
        multiply(1, 1, 2)
        result[...] = collect(0, batch)
        wait_flat(13)
        multiply(1, 1, -3)
        wait_flat(14)
        multiply(1, 1, 3)
        for s in range(2):
            wait_flat(15 + s, near)
            multiply(1, 1, HOPS, s * near, near)
            finish(1, s * near, near)

    @pl.when(h == 1)
    def _():
        def number_of(b, i, s):
            return i if b == 0 else batch + i + s

        def flat_ref(p, j, way, place):
            if j < HOPS:
                return flat.at[place, pl.ds(p * piece, piece)]
            return flat.at[place, pl.ds(p * piece + way * (piece // 2), piece // 2)]

        def send_flat(p, j, way):
            ref = flat_ref(p, j, way, place_of(j - 1, way))
            recv = flat_recv.at[p, way * HOPS + j - 1]
            remote(ref, ref, out_send.at[4 if j < HOPS else 5], recv, toward_way(way)).start()

        def hop(j):
            for p in range(pieces):
                for way in range(2):
                    ref = flat_ref(p, j, way, place_of(j, way))
                    recv = flat_recv.at[p, way * HOPS + j - 1]
                    remote(ref, ref, out_send.at[4], recv, toward_way(way)).wait_recv()
                    if j < HOPS:
                        send_flat(p, j + 1, way)

        def send_rows(b, i):
            place = place_at(offset[i])
            for g in range(max(1, b * batch), (b + 1) * batch):
                recv = many_recv.at[number_of(b, i, (g - batch) // near if b == 1 and i == RING - 1 else 0)]
                remote(
                    send.at[place, rows_of(g)], x.at[1, place, rows_of(g)], out_send.at[0], recv,
                    (toward(g), lev),
                ).start()

        def arrived(b, i, s=None):
            place = place_at(offset[i])
            start, count = (b * batch, batch) if s is None else (b * batch + s * near, near)
            number = number_of(b, i, s or 0)
            base = max(1, start)
            wait_bytes(
                x.at[1, place, pl.ds(base * cap, (start + count - base) * cap)], many_recv.at[number]
            )
            ref = x.at[1, place, pl.ds(start * cap, count * cap)]
            remote(ref, ref, out_send.at[2], flat_twin.at[number], (c, twin)).start()

        for p in range(pieces):
            for way in range(2):
                send_flat(p, 1, way)
        def pass_on(b, *numbers):
            for i in numbers:
                route(place_at(offset[i]), b, 1)
                send_rows(b, i)

        pass_on(0, 0)
        make_pick()
        moved_copy.start()
        hop(1)
        pass_on(0, 1, 2)
        pass_on(1, 0)
        send_offsets()
        arrived(0, 0)
        wait_weights()
        multiply(0, 1, 0, fresh=True)
        hop(2)
        pass_on(0, 3, 4)
        pass_on(1, 1)
        arrived(0, 1)
        arrived(0, 2)
        multiply_two(0, 1, 1)
        hop(3)
        pass_on(0, 5, 6)
        pass_on(1, 2)
        arrived(0, 3)
        arrived(0, 4)
        wait_padded(0, 1, 0, batch)
        multiply(0, 0, 0)
        hop(HOPS)
        pass_on(0, 7)
        pass_on(1, 3, 4)
        arrived(0, 5)
        arrived(0, 6)
        pass_on(1, 5, 6)
        multiply_two(0, 1, 2)
        pass_on(1, 7)
        wait_padded(1, 2, 0, batch)
        multiply_two(0, 0, 1)
        arrived(0, 7)
        multiply_two(0, 1, 3)
        arrived(1, 0)
        wait_padded(2, 2, 0, batch)
        multiply_two(0, 0, 2)
        multiply(0, 1, HOPS)
        arrived(1, 1)
        arrived(1, 2)
        wait_padded(3, 2, 0, batch)
        multiply_two(0, 0, 3)
        wait_padded(HOPS, 1, 0, batch)
        multiply(0, 0, HOPS)
        finish(0, 0, batch)
        multiply(1, 1, 0, fresh=True)
        for i in (3, 4):
            arrived(1, i)
        multiply_two(1, 1, 1)
        wait_padded(5, 1, batch, batch)
        multiply(1, 0, 0)
        for i in (5, 6):
            arrived(1, i)
        multiply_two(1, 1, 2)
        arrived(1, RING - 1, 0)
        wait_padded(6, 2, batch, batch)
        multiply_two(1, 0, 1)
        arrived(1, RING - 1, 1)
        multiply_two(1, 1, 3)
        wait_padded(7, 2, batch, batch)
        multiply_two(1, 0, 2)
        multiply(1, 1, HOPS)
        result[...] = collect(0, batch)
        wait_padded(8, 2, batch, batch)
        multiply_two(1, 0, 3)
        for s in range(2):
            wait_padded(5 + HOPS + s, 1, batch + s * near, near)
            multiply(1, 0, HOPS, s * near, near)
            finish(1, s * near, near)

    result[...] += collect(batch, near)
    total = result[...] + collect(batch + near, near)
    sources[...] = total.astype(BF16)

    moved_copy.wait()
    rest = pl.ds(cap, (groups - 1) * cap)

    @pl.when(h == 0)
    def _():
        wait_bytes(send.at[0, rest], out_send.at[0])
        wait_bytes(x.at[0, pl.ds(0, 2 * HOPS - 2)], out_send.at[4])
        wait_bytes(x.at[0, 0], out_send.at[5])

    @pl.when(h == 1)
    def _():
        wait_bytes(send.at[:, rest], out_send.at[0])
        wait_bytes(flat.at[pl.ds(0, 2 * HOPS - 2)], out_send.at[4])
        wait_bytes(flat.at[0], out_send.at[5])

    wait_bytes(off_recv.at[pl.ds(1, groups - 1)], out_send.at[1])
    wait_bytes(x.at[0], out_send.at[2])
    wait_bytes(back_send.at[rest], out_send.at[3])


def shards(
    populations, face_speed, cell_class, class_offset, rate_matrix, slope_matrix, rate_scale, slope_scale
):
    rows, width = populations.shape
    groups = SIDE * SIDE
    cap = 2 * rows // groups
    slots = groups * cap
    vmem = pl.BlockSpec(memory_space=pltpu.VMEM)
    hbm = pl.BlockSpec(memory_space=pl.ANY)
    dma = pltpu.SemaphoreType.DMA
    narrow_sources, transported = pl.pallas_call(
        kernel,
        out_shape=(
            jax.ShapeDtypeStruct((rows, width), BF16), jax.ShapeDtypeStruct((rows, width), F32)
        ),
        in_specs=[vmem, vmem, vmem, hbm, hbm, hbm, vmem, vmem],
        out_specs=(vmem, hbm),
        scratch_shapes=[
            pltpu.VMEM((rows + 16, width), F32),
            pltpu.VMEM((2 * RING, width, width), BF16),
            pltpu.VMEM((2 * RING, width, width), BF16),
            pltpu.VMEM((2, RING, slots, width), BF16),
            pltpu.VMEM((RING, rows, width), BF16),
            pltpu.VMEM((RING, slots, width), BF16),
            pltpu.VMEM((groups // 2, 16, 128), BF16),
            pltpu.VMEM((groups, 16, 128), BF16),
            pltpu.VMEM((slots, width), BF16),
            pltpu.VMEM((slots, width), BF16),
            pltpu.VMEM((slots, rows), BF16),
            pltpu.VMEM((rows, slots), BF16),
            pltpu.VMEM((rows, width), F32),
            pltpu.VMEM((2, slots, width), F32),
            pltpu.VMEM((rows, width), F32),
            dma((3,)),
            dma((2,)),
            dma((2,)),
            dma((6,)),
            dma((groups,)),
            dma((2 * RING + 1,)),
            dma((groups,)),
            dma((groups, RING)),
            dma((4, RING)),
            dma((11,)),
            dma((2 * RING + 1,)),
            dma((groups,)),
        ],
        compiler_params=pltpu.CompilerParams(
            collective_id=0, has_side_effects=True, vmem_limit_bytes=60 * 1024 * 1024
        ),
    )(
        cell_class.reshape(4, -1), class_offset, face_speed,
        populations, rate_matrix, slope_matrix, rate_scale, slope_scale,
    )
    sources = narrow_sources.astype(F32)
    return sources, transported + 0.5 * sources


def solution(mesh):
    in_specs = (
        P("cells", "levels"),
        P(),
        P("cells", None),
        P("cells"),
        P("cells", "levels", None),
        P("cells", "levels", None),
        P("cells", "levels"),
        P("cells", "levels"),
    )
    out_specs = (P("cells", "levels"), P("cells", "levels"))
    return jax.shard_map(shards, mesh=mesh, in_specs=in_specs, out_specs=out_specs, check_vma=False)
```

time: 85.9 us -> 69.3 us (0.81)
  the two profiles are of different devices: /device:TPU:14 before, /device:TPU:1 now
where the time goes in v2:
time: 69.3 us; the launch traced here: 69.1 us
  Pallas kernels  66.4 us (96%)
  other arithmetic  2.15 us (3%)
    pallas_call x1, Pallas kernels, shards(): pl.pallas_call(kernel, out_shape=(jax.ShapeDtypeStruct((rows, width), BF1...  66.4 us
    add x1, other arithmetic, shards(): return (sources, transported + 0.5 * sources)  2.15 us

profile of v2, /device:TPU:1, one launch (start us, length us, event | category | flops | bytes accessed | tf_op | source)
XLA Modules:
  0.0 69.1 jit_solution(8355486994771468561)
XLA Ops:
  0.6 66.4 %shard_map.95 = (bf16[512,256]{1,0:T(8,128)(2,1)}, f32[512,256]{1,0:T(8,128)}) custom-call(s32[4,128]{1,0:T(4,128)} %bitcast.1, bf16[512]{0:T(512)(128)(2,1)} %off4.1, f32[8193]{0:T(1024)} %speeds.1, f32[512,256]{1,0:T(8,128)} %pop.1, bf16[1,256,4096]{2,1,0:T(8,128)(2,1)} %rate.1, bf16[1,256,4096]{2,1,0:T(8,128)(2,1)} %slope.1, f32[1,256]{1,0:T(1,128)} %rate_gain.1, ...), custom_call_target="tpu_custom_call" | custom-call | tf_op jit(solution)/shard_map/pallas_call | solution.py:608
  67.0 2.2 %multiply_add_fusion = (f32[512,256]{1,0:T(8,128)}, f32[512,256]{1,0:T(8,128)}) fusion(f32[512,256]{1,0:T(8,128)} %get-tuple-element.5, bf16[512,256]{1,0:T(8,128)(2,1)} %get-tuple-element.4), kind=kLoop, calls=%fused_computation | loop fusion | flops 393216 | bytes 1835008 | tf_op jit(solution)/shard_map/add | solution.py:652

commit v3 on v2

--- a/solution.py
+++ b/solution.py
@@ -36,8 +36,8 @@
 
 
 def kernel(
-    cls4, off4, speeds, pop, rate, slope, rate_gain, slope_gain, sources, transported,
-    pad, wr, ws, x, flat, send, off_send, off_recv, back_send, back, take, pick, moved, acc, result,
+    cls_in, off_in, speeds_in, pop, rate, slope, rate_gain_in, slope_gain_in, sources, transported,
+    cls4, off4, speeds, rate_gain, slope_gain, pad, wr, ws, x, flat, send, off_send, off_recv, back_send, back, take, pick, moved, acc, result,
     local_sem, halo_send, halo_recv, out_send, row_recv, many_recv, offs_recv, ring_recv, flat_recv,
     padded_twin, flat_twin, back_recv,
 ):
@@ -75,12 +75,25 @@
         pl.semaphore_signal(barrier, inc=1, device_id=(c, peer), device_id_type=MESH)
 
     pop_copy = pltpu.make_async_copy(pop, pad.at[pl.ds(8, rows)], local_sem.at[0])
+    small = [
+        pltpu.make_async_copy(src, dst, local_sem.at[3 + i])
+        for i, (src, dst) in enumerate((
+            (cls_in, cls4), (off_in, off4), (speeds_in, speeds),
+            (rate_gain_in, rate_gain), (slope_gain_in, slope_gain),
+        ))
+    ]
+    for copy in small[:3]:
+        copy.start()
     pop_copy.start()
+    for copy in small[3:]:
+        copy.start()
     for i in range(2 * RING):
         lanes = pl.ds(i * width, width)
         pltpu.make_async_copy(rate.at[0, :, lanes], wr.at[i], local_sem.at[1]).start()
         pltpu.make_async_copy(slope.at[0, :, lanes], ws.at[i], local_sem.at[2]).start()
 
+    for copy in small[:3]:
+        copy.wait()
     cls = jnp.concatenate([cls4[pl.ds(q, 1), :] for q in range(4)], axis=1)
     hot = (iota((groups, rows), 0) == cls).astype(F32)
     earlier = (iota((rows, rows), 0) < iota((rows, rows), 1)).astype(F32).astype(BF16)
@@ -125,6 +138,22 @@
             (iota((4 * cap, rows), 0) + 4 * cap * q == slot).astype(F32).astype(BF16)
         )
 
+    def transport(start, count):
+        q, r = start // quarter, start % quarter
+        a = pad[pl.ds(start + 7, count), :]
+        b = pad[pl.ds(start + 8, count), :]
+        d = pad[pl.ds(start + 9, count), :]
+        lower = 0.5 * column(q)[r : r + count] * (a + b) - 0.625 * (b - a)
+        upper = 0.5 * column(4 + q)[r : r + count] * (b + d) - 0.625 * (d - b)
+        t = b + 0.4 * (lower - upper)
+        moved[pl.ds(start, count), :] = t
+        flat[z, pl.ds(start, count), :] = t.astype(BF16)
+
+    edge = 16
+    transport(edge, quarter - edge)
+    transport(quarter, quarter)
+    transport(2 * quarter, quarter)
+    transport(3 * quarter, quarter - edge)
     up.wait()
     down.wait()
 
@@ -136,15 +165,8 @@
     def _():
         pad[pl.ds(rows + 8, 8), :] = jnp.zeros((8, width), F32)
 
-    for q in range(4):
-        a = pad[pl.ds(q * quarter + 7, quarter), :]
-        b = pad[pl.ds(q * quarter + 8, quarter), :]
-        d = pad[pl.ds(q * quarter + 9, quarter), :]
-        lower = 0.5 * column(q) * (a + b) - 0.625 * (b - a)
-        upper = 0.5 * column(4 + q) * (b + d) - 0.625 * (d - b)
-        t = b + 0.4 * (lower - upper)
-        moved[pl.ds(q * quarter, quarter), :] = t
-        flat[z, pl.ds(q * quarter, quarter), :] = t.astype(BF16)
+    transport(0, edge)
+    transport(rows - edge, edge)
 
     offsets = jnp.broadcast_to(
         jnp.concatenate([o4[q : q + 1] for q in range(4)], axis=1), (16, rows)
@@ -207,6 +229,8 @@
     def wait_weights():
         wait_bytes(wr, local_sem.at[1])
         wait_bytes(ws, local_sem.at[2])
+        for copy in small[3:]:
+            copy.wait()
 
     def multiply(b, role, shift, start=0, count=batch, fresh=False):
         place = place_at(shift)
@@ -312,138 +336,62 @@
             for g in range(max(1, b * batch), (b + 1) * batch):
                 row_copy(g, (toward(g), lev)).start()
 
+        def group_loop(k, f, steps):
+            def body(g):
+                f(g)
+                for i, step in steps.items():
+                    pl.when(g == k * near + i)(step)
+
+            each(k * near, (k + 1) * near, body)
+
+        def enter(k):
+            group_loop(k, lambda g: first(g, k // 2), {})
+
+        def turn(k, j, steps):
+            group_loop(k, lambda g: middle(g, k // 2, j), steps)
+
+        def leave(k, steps):
+            group_loop(k, lambda g: last(g, HOPS if k < 2 else 3 + HOPS + k), steps)
+
+        def own(b, shift, fresh=False):
+            return lambda: multiply(b, 0, shift, fresh=fresh)
+
+        def other(b, i):
+            def step():
+                wait_flat(b * batch + i)
+                multiply(b, 1, offset[i])
+
+            return step
+
         send_rows(0)
         first(0, 0)
         make_pick()
         moved_copy.start()
         each(1, near, lambda g: first(g, 0))
-
-        def start_up(g):
-            first(g + near, 0)
-            middle(g, 0, 1)
-
-        each(0, near, start_up)
+        turn(0, 1, {})
         send_rows(1)
+        enter(1)
+        turn(0, 2, {})
+        wait_weights()
+        turn(1, 1, {3: own(0, 0, True)})
+        turn(0, 3, {1: own(0, -1), 3: own(0, 1)})
         send_offsets()
-        each(near, batch, lambda g: middle(g, 0, 1))
-        wait_weights()
-        multiply(0, 0, 0, fresh=True)
-
-        def turn_2(i):
-            middle(i, 0, 2)
-            when(i, 1, lambda: multiply(0, 0, -1))
-            when(i, 3, lambda: multiply(0, 0, 1))
-
-        each(0, batch, turn_2)
-
-        def turn_3(i):
-            middle(i, 0, 3)
-            when(i, 1, lambda: multiply(0, 0, -2))
-            when(i, 3, lambda: multiply(0, 0, 2))
-
-            @pl.when(i == 5)
-            def _():
-                wait_flat(0)
-                multiply(0, 1, 0)
-
-        each(0, batch, turn_3)
-        each(batch, groups, lambda g: first(g, 1))
-
-        def turn_last(i):
-            last(i, HOPS)
-            when(i, 1, lambda: multiply(0, 0, -3))
-            when(i, 2, lambda: multiply(0, 0, 3))
-
-            @pl.when(i == 4)
-            def _():
-                wait_flat(1)
-                multiply(0, 1, -1)
-
-            @pl.when(i == 6)
-            def _():
-                wait_flat(2)
-                multiply(0, 1, 1)
-
-        each(0, batch, turn_last)
-
-        def turn_over(i):
-            middle(batch + i, 1, 1)
-            when(i, 0, lambda: multiply(0, 0, HOPS))
-
-            @pl.when(i == 2)
-            def _():
-                wait_flat(3)
-                multiply(0, 1, -2)
-
-            @pl.when(i == 4)
-            def _():
-                wait_flat(4)
-                multiply(0, 1, 2)
-
-            when(i, 6, lambda: multiply(1, 0, 0, fresh=True))
-
-        each(0, batch, turn_over)
-
-        def turn_6(i):
-            middle(batch + i, 1, 2)
-
-            @pl.when(i == 0)
-            def _():
-                wait_flat(5)
-                multiply(0, 1, -3)
-
-            @pl.when(i == 2)
-            def _():
-                wait_flat(6)
-                multiply(0, 1, 3)
-
-            @pl.when(i == 4)
-            def _():
-                wait_flat(7)
-                multiply(0, 1, HOPS)
-                finish(0, 0, batch)
-
-            when(i, 5, lambda: multiply(1, 0, -1))
-            when(i, 6, lambda: multiply(1, 0, 1))
-
-        each(0, batch, turn_6)
-
-        def turn_7(i):
-            middle(batch + i, 1, 3)
-
-            @pl.when(i == 0)
-            def _():
-                wait_flat(8)
-                multiply(1, 1, 0)
-
-            when(i, 1, lambda: multiply(1, 0, -2))
-            when(i, 2, lambda: multiply(1, 0, 2))
-
-            @pl.when(i == 4)
-            def _():
-                wait_flat(9)
-                multiply(1, 1, -1)
-
-            @pl.when(i == 6)
-            def _():
-                wait_flat(10)
-                multiply(1, 1, 1)
-
-        each(0, batch, turn_7)
-        each(0, 2, lambda i: multiply(1, 0, 3 * (2 * i - 1)))
-        each(batch, batch + near, lambda g: last(g, 5 + HOPS))
-        each(batch + near, groups, lambda g: last(g, 5 + HOPS + 1))
-        multiply(1, 0, HOPS)
-        wait_flat(11)
-        multiply(1, 1, -2)
-        wait_flat(12)
-        multiply(1, 1, 2)
-        result[...] = collect(0, batch)
-        wait_flat(13)
-        multiply(1, 1, -3)
-        wait_flat(14)
-        multiply(1, 1, 3)
+        turn(1, 2, {1: other(0, 0)})
+        enter(2)
+        enter(3)
+        leave(0, {})
+        turn(1, 3, {1: other(0, 1), 3: other(0, 2)})
+        turn(2, 1, {1: own(0, -2), 3: own(0, 2)})
+        turn(3, 1, {0: other(0, 3), 2: other(0, 4)})
+        leave(1, {0: own(0, -3), 2: own(0, 3)})
+        turn(2, 2, {0: other(0, 5), 1: own(0, HOPS), 3: other(0, 6)})
+        turn(3, 2, {0: own(1, 0, True), 1: own(1, -1), 2: own(1, 1), 3: other(1, 0)})
+        turn(2, 3, {0: other(1, 1), 2: other(1, 2)})
+        turn(3, 3, {0: other(0, 7), 1: lambda: finish(0, 0, batch), 2: own(1, -2), 3: own(1, 2)})
+        leave(2, {0: other(1, 3), 2: other(1, 4)})
+        leave(3, {0: own(1, -3), 1: own(1, 3), 2: other(1, 5), 3: other(1, 6)})
         for s in range(2):
+            multiply(1, 0, HOPS, s * near, near)
             wait_flat(15 + s, near)
             multiply(1, 1, HOPS, s * near, near)
             finish(1, s * near, near)
@@ -463,8 +411,10 @@
             recv = flat_recv.at[p, way * HOPS + j - 1]
             remote(ref, ref, out_send.at[4 if j < HOPS else 5], recv, toward_way(way)).start()
 
-        def hop(j):
+        def hop(j, between=None):
             for p in range(pieces):
+                if p == 2 and between is not None:
+                    between()
                 for way in range(2):
                     ref = flat_ref(p, j, way, place_of(j, way))
                     recv = flat_recv.at[p, way * HOPS + j - 1]
@@ -503,9 +453,8 @@
         pass_on(0, 0)
         make_pick()
         moved_copy.start()
-        hop(1)
+        hop(1, lambda: pass_on(1, 0))
         pass_on(0, 1, 2)
-        pass_on(1, 0)
         send_offsets()
         arrived(0, 0)
         wait_weights()
@@ -519,58 +468,58 @@
         hop(3)
         pass_on(0, 5, 6)
         pass_on(1, 2)
-        arrived(0, 3)
-        arrived(0, 4)
         wait_padded(0, 1, 0, batch)
         multiply(0, 0, 0)
         hop(HOPS)
         pass_on(0, 7)
+        arrived(0, 3)
+        arrived(0, 4)
         pass_on(1, 3, 4)
+        multiply_two(0, 1, 2)
+        pass_on(1, 5, 6)
+        wait_padded(1, 2, 0, batch)
+        multiply_two(0, 0, 1)
+        pass_on(1, 7)
         arrived(0, 5)
         arrived(0, 6)
-        pass_on(1, 5, 6)
-        multiply_two(0, 1, 2)
-        pass_on(1, 7)
-        wait_padded(1, 2, 0, batch)
-        multiply_two(0, 0, 1)
-        arrived(0, 7)
         multiply_two(0, 1, 3)
-        arrived(1, 0)
         wait_padded(2, 2, 0, batch)
         multiply_two(0, 0, 2)
+        arrived(0, 7)
+        arrived(1, 0)
         multiply(0, 1, HOPS)
-        arrived(1, 1)
-        arrived(1, 2)
         wait_padded(3, 2, 0, batch)
         multiply_two(0, 0, 3)
         wait_padded(HOPS, 1, 0, batch)
         multiply(0, 0, HOPS)
         finish(0, 0, batch)
+        arrived(1, 1)
+        arrived(1, 2)
         multiply(1, 1, 0, fresh=True)
-        for i in (3, 4):
-            arrived(1, i)
-        multiply_two(1, 1, 1)
         wait_padded(5, 1, batch, batch)
         multiply(1, 0, 0)
-        for i in (5, 6):
-            arrived(1, i)
-        multiply_two(1, 1, 2)
-        arrived(1, RING - 1, 0)
+        arrived(1, 3)
+        arrived(1, 4)
+        multiply_two(1, 1, 1)
         wait_padded(6, 2, batch, batch)
         multiply_two(1, 0, 1)
-        arrived(1, RING - 1, 1)
-        multiply_two(1, 1, 3)
+        arrived(1, 5)
+        arrived(1, 6)
+        multiply_two(1, 1, 2)
+        arrived(1, 7, 0)
         wait_padded(7, 2, batch, batch)
         multiply_two(1, 0, 2)
-        multiply(1, 1, HOPS)
-        result[...] = collect(0, batch)
+        arrived(1, 7, 1)
+        multiply_two(1, 1, 3)
         wait_padded(8, 2, batch, batch)
         multiply_two(1, 0, 3)
         for s in range(2):
+            multiply(1, 1, HOPS, s * near, near)
             wait_padded(5 + HOPS + s, 1, batch + s * near, near)
             multiply(1, 0, HOPS, s * near, near)
             finish(1, s * near, near)
 
+    result[...] = collect(0, batch)
     result[...] += collect(batch, near)
     total = result[...] + collect(batch + near, near)
     sources[...] = total.astype(BF16)
@@ -610,9 +559,14 @@
         out_shape=(
             jax.ShapeDtypeStruct((rows, width), BF16), jax.ShapeDtypeStruct((rows, width), F32)
         ),
-        in_specs=[vmem, vmem, vmem, hbm, hbm, hbm, vmem, vmem],
+        in_specs=[hbm] * 8,
         out_specs=(vmem, hbm),
         scratch_shapes=[
+            pltpu.VMEM((4, rows // 4), I32),
+            pltpu.VMEM(class_offset.shape, BF16),
+            pltpu.VMEM(face_speed.shape, F32),
+            pltpu.VMEM((1, width), F32),
+            pltpu.VMEM((1, width), F32),
             pltpu.VMEM((rows + 16, width), F32),
             pltpu.VMEM((2 * RING, width, width), BF16),
             pltpu.VMEM((2 * RING, width, width), BF16),
@@ -628,7 +582,7 @@
             pltpu.VMEM((rows, width), F32),
             pltpu.VMEM((2, slots, width), F32),
             pltpu.VMEM((rows, width), F32),
-            dma((3,)),
+            dma((8,)),
             dma((2,)),
             dma((2,)),
             dma((6,)),

time: 69.3 us -> 65 us (0.938)
  Pallas kernels: 66.4 us -> 61.5 us
    pallas_call x1, Pallas kernels: 66.4 us -> 61.5 us  [shards(): pl.pallas_call(kernel, out_shape=(jax.ShapeDtypeStruct((rows, width), BF1...]
where the time goes in v3:
time: 65 us; the launch traced here: 64.2 us
  Pallas kernels  61.5 us (95%)
  other arithmetic  2.15 us (3%)
    pallas_call x1, Pallas kernels, shards(): pl.pallas_call(kernel, out_shape=(jax.ShapeDtypeStruct((rows, width), BF1...  61.5 us
    add x1, other arithmetic, shards(): return (sources, transported + 0.5 * sources)  2.15 us

profile of v3, /device:TPU:1, one launch (start us, length us, event | category | flops | bytes accessed | tf_op | source)
XLA Modules:
  0.0 64.2 jit_solution(8981447590632839404)
XLA Ops:
  0.6 61.5 %shard_map.95 = (bf16[512,256]{1,0:T(8,128)(2,1)}, f32[512,256]{1,0:T(8,128)}) custom-call(s32[4,128]{1,0:T(4,128)} %bitcast.1, bf16[512]{0:T(512)(128)(2,1)} %off_in.1, f32[8193]{0:T(1024)} %speeds_in.1, f32[512,256]{1,0:T(8,128)} %pop.1, bf16[1,256,4096]{2,1,0:T(8,128)(2,1)} %rate.1, bf16[1,256,4096]{2,1,0:T(8,128)(2,1)} %slope.1, f32[1,256]{1,0:T(1,128)} %rate_gain_in.1, ...), custom_call_target="tpu_custom_call" | custom-call | tf_op jit(solution)/shard_map/pallas_call | solution.py:557
  62.1 2.2 %multiply_add_fusion = (f32[512,256]{1,0:T(8,128)}, f32[512,256]{1,0:T(8,128)}) fusion(f32[512,256]{1,0:T(8,128)} %get-tuple-element.5, bf16[512,256]{1,0:T(8,128)(2,1)} %get-tuple-element.4), kind=kLoop, calls=%fused_computation | loop fusion | flops 393216 | bytes 1835008 | tf_op jit(solution)/shard_map/add | solution.py:606

commit v4 on v3

--- a/solution.py
+++ b/solution.py
@@ -38,8 +38,7 @@
 def kernel(
     cls_in, off_in, speeds_in, pop, rate, slope, rate_gain_in, slope_gain_in, sources, transported,
     cls4, off4, speeds, rate_gain, slope_gain, pad, wr, ws, x, flat, send, off_send, off_recv, back_send, back, take, pick, moved, acc, result,
-    local_sem, halo_send, halo_recv, out_send, row_recv, many_recv, offs_recv, ring_recv, flat_recv,
-    padded_twin, flat_twin, back_recv,
+    local_sem, halo_send, halo_recv, out_send, arrive, ring_recv, twin_recv, offs_recv, back_recv,
 ):
     rows, width = result.shape
     groups = SIDE * SIDE
@@ -206,8 +205,11 @@
             if b == 0 and q == 0:
                 x[own_role, place, pl.ds(0, cap), :] = got[:cap]
 
+    def part_of(g):
+        return max(0, g // near - 1)
+
     def off_copy(g, device):
-        return remote(off_send.at[g // 2], off_recv.at[g], out_send.at[1], offs_recv.at[g], device)
+        return remote(off_send.at[g // 2], off_recv.at[g], out_send.at[1], offs_recv.at[part_of(g)], device)
 
     def send_offsets():
         got = nt(offsets, take[...]).astype(BF16)
@@ -249,13 +251,13 @@
 
     def back_copy(g, device):
         return remote(
-            back_send.at[rows_of(g)], back.at[rows_of(g)], out_send.at[3], back_recv.at[g], device
+            back_send.at[rows_of(g)], back.at[rows_of(g)], out_send.at[3], back_recv.at[part_of(g)], device
         )
 
     def finish(b, start, count):
         base = b * batch + start
-        for g in range(max(1, base), base + count):
-            off_copy(g, (c, lev)).wait_recv()
+        start = max(1, base)
+        wait_bytes(off_recv.at[pl.ds(start, base + count - start)], offs_recv.at[part_of(base)])
         low = iota((1, 2 * cap), 1) < cap
         o = [
             jnp.where(low, off_recv[g, 0:1, :].astype(F32), off_recv[g + 1, 0:1, :].astype(F32))
@@ -272,22 +274,22 @@
             back_copy(g, (origin(g), lev)).start()
 
     def collect(base, count):
-        for g in range(max(1, base), base + count):
-            back_copy(g, (c, lev)).wait_recv()
+        start = max(1, base)
+        wait_bytes(back.at[pl.ds(start * cap, (base + count - start) * cap)], back_recv.at[part_of(base)])
         span = pl.ds(base * cap, count * cap)
         return jnp.dot(pick[:, span], back[span, :], preferred_element_type=F32)
 
     def wait_padded(number, chunks, start, count):
-        wait_bytes(x.at[0, pl.ds(0, chunks), pl.ds(start * cap, count * cap)], padded_twin.at[number])
+        wait_bytes(x.at[0, pl.ds(0, chunks), pl.ds(start * cap, count * cap)], twin_recv.at[number])
 
     def wait_flat(number, count=batch):
-        wait_bytes(x.at[1, 0, pl.ds(0, count * cap)], flat_twin.at[number])
+        wait_bytes(x.at[1, 0, pl.ds(0, count * cap)], twin_recv.at[number])
 
     @pl.when(h == 0)
     def _():
         def row_copy(g, device):
             return remote(
-                send.at[z, rows_of(g)], x.at[0, z, rows_of(g)], out_send.at[0], row_recv.at[g], device
+                send.at[z, rows_of(g)], x.at[0, z, rows_of(g)], out_send.at[0], arrive.at[g], device
             )
 
         def span_of(g, j, way):
@@ -298,19 +300,19 @@
         def ring_ref(g, j, way, place):
             return x.at[0, place, span_of(g, j, way)]
 
-        def wait_ring(g, j, way):
-            ref = ring_ref(g, j, way, place_of(j, way))
-            recv = ring_recv.at[g, way * HOPS + j - 1]
-            remote(ref, ref, out_send.at[2], recv, toward_way(way)).wait_recv()
+        def wait_ring(g, j):
+            ref = x.at[0, pl.ds(0, 2), rows_of(g)] if j < HOPS else x.at[0, 0, rows_of(g)]
+            wait_bytes(ref, ring_recv.at[g, j - 1])
 
         def send_ring(g, j, way):
             ref = ring_ref(g, j, way, place_of(j - 1, way))
-            recv = ring_recv.at[g, way * HOPS + j - 1]
-            remote(ref, ref, out_send.at[4 if j < HOPS else 5], recv, toward_way(way)).start()
+            remote(
+                ref, ref, out_send.at[4 if j < HOPS else 5], ring_recv.at[g, j - 1], toward_way(way)
+            ).start()
 
         def send_twin(g, place, number):
             ref = x.at[0, place, rows_of(g)]
-            remote(ref, ref, out_send.at[2], padded_twin.at[number], (c, twin)).start()
+            remote(ref, ref, out_send.at[2], twin_recv.at[number], (c, twin)).start()
 
         def first(g, b):
             if not isinstance(g, int):
@@ -321,14 +323,13 @@
             send_twin(g, z, 5 * b)
 
         def middle(g, b, j):
+            wait_ring(g, j)
             for way in range(2):
-                wait_ring(g, j, way)
                 send_ring(g, j + 1, way)
                 send_twin(g, place_of(j, way), 5 * b + j)
 
         def last(g, number):
-            for way in range(2):
-                wait_ring(g, HOPS, way)
+            wait_ring(g, HOPS)
             send_twin(g, place_of(HOPS, 0), number)
 
         def send_rows(b):
@@ -389,13 +390,29 @@
         turn(2, 3, {0: other(1, 1), 2: other(1, 2)})
         turn(3, 3, {0: other(0, 7), 1: lambda: finish(0, 0, batch), 2: own(1, -2), 3: own(1, 2)})
         leave(2, {0: other(1, 3), 2: other(1, 4)})
-        leave(3, {0: own(1, -3), 1: own(1, 3), 2: other(1, 5), 3: other(1, 6)})
-        for s in range(2):
+        def half_own(s):
+            multiply(1, 0, -3, s * near, near)
+            multiply(1, 0, 3, s * near, near)
+
+        def half_other(s):
+            if s == 0:
+                wait_flat(batch + 5)
+                wait_flat(batch + 6)
+            multiply(1, 1, -3, s * near, near)
+            multiply(1, 1, 3, s * near, near)
+
+        def half_end(s):
             multiply(1, 0, HOPS, s * near, near)
             wait_flat(15 + s, near)
             multiply(1, 1, HOPS, s * near, near)
             finish(1, s * near, near)
 
+        leave(3, {
+            0: lambda: half_own(0), 1: lambda: half_other(0), 2: lambda: half_end(0), 3: lambda: half_own(1)
+        })
+        half_other(1)
+        half_end(1)
+
     @pl.when(h == 1)
     def _():
         def number_of(b, i, s):
@@ -408,24 +425,25 @@
 
         def send_flat(p, j, way):
             ref = flat_ref(p, j, way, place_of(j - 1, way))
-            recv = flat_recv.at[p, way * HOPS + j - 1]
-            remote(ref, ref, out_send.at[4 if j < HOPS else 5], recv, toward_way(way)).start()
+            remote(
+                ref, ref, out_send.at[4 if j < HOPS else 5], ring_recv.at[p, j - 1], toward_way(way)
+            ).start()
 
         def hop(j, between=None):
             for p in range(pieces):
                 if p == 2 and between is not None:
                     between()
-                for way in range(2):
-                    ref = flat_ref(p, j, way, place_of(j, way))
-                    recv = flat_recv.at[p, way * HOPS + j - 1]
-                    remote(ref, ref, out_send.at[4], recv, toward_way(way)).wait_recv()
-                    if j < HOPS:
+                span = pl.ds(p * piece, piece)
+                ref = flat.at[pl.ds(0, 2), span] if j < HOPS else flat.at[0, span]
+                wait_bytes(ref, ring_recv.at[p, j - 1])
+                if j < HOPS:
+                    for way in range(2):
                         send_flat(p, j + 1, way)
 
         def send_rows(b, i):
             place = place_at(offset[i])
             for g in range(max(1, b * batch), (b + 1) * batch):
-                recv = many_recv.at[number_of(b, i, (g - batch) // near if b == 1 and i == RING - 1 else 0)]
+                recv = arrive.at[number_of(b, i, (g - batch) // near if b == 1 and i == RING - 1 else 0)]
                 remote(
                     send.at[place, rows_of(g)], x.at[1, place, rows_of(g)], out_send.at[0], recv,
                     (toward(g), lev),
@@ -437,10 +455,10 @@
             number = number_of(b, i, s or 0)
             base = max(1, start)
             wait_bytes(
-                x.at[1, place, pl.ds(base * cap, (start + count - base) * cap)], many_recv.at[number]
+                x.at[1, place, pl.ds(base * cap, (start + count - base) * cap)], arrive.at[number]
             )
             ref = x.at[1, place, pl.ds(start * cap, count * cap)]
-            remote(ref, ref, out_send.at[2], flat_twin.at[number], (c, twin)).start()
+            remote(ref, ref, out_send.at[2], twin_recv.at[number], (c, twin)).start()
 
         for p in range(pieces):
             for way in range(2):
@@ -482,19 +500,19 @@
         pass_on(1, 7)
         arrived(0, 5)
         arrived(0, 6)
+        arrived(1, 0)
         multiply_two(0, 1, 3)
         wait_padded(2, 2, 0, batch)
         multiply_two(0, 0, 2)
-        arrived(0, 7)
-        arrived(1, 0)
-        multiply(0, 1, HOPS)
+        arrived(1, 1)
+        arrived(1, 2)
         wait_padded(3, 2, 0, batch)
         multiply_two(0, 0, 3)
+        arrived(0, 7)
+        multiply(0, 1, HOPS)
         wait_padded(HOPS, 1, 0, batch)
         multiply(0, 0, HOPS)
         finish(0, 0, batch)
-        arrived(1, 1)
-        arrived(1, 2)
         multiply(1, 1, 0, fresh=True)
         wait_padded(5, 1, batch, batch)
         multiply(1, 0, 0)
@@ -586,14 +604,11 @@
             dma((2,)),
             dma((2,)),
             dma((6,)),
-            dma((groups,)),
             dma((2 * RING + 1,)),
-            dma((groups,)),
-            dma((groups, RING)),
-            dma((4, RING)),
-            dma((11,)),
+            dma((groups, HOPS)),
             dma((2 * RING + 1,)),
-            dma((groups,)),
+            dma((3,)),
+            dma((3,)),
         ],
         compiler_params=pltpu.CompilerParams(
             collective_id=0, has_side_effects=True, vmem_limit_bytes=60 * 1024 * 1024

time: 65 us -> 62.8 us (0.966)
  Pallas kernels: 61.5 us -> 59.9 us
    pallas_call x1, Pallas kernels: 61.5 us -> 59.9 us  [shards(): pl.pallas_call(kernel, out_shape=(jax.ShapeDtypeStruct((rows, width), BF1...]
where the time goes in v4:
time: 62.8 us; the launch traced here: 62.7 us
  Pallas kernels  59.9 us (95%)
  other arithmetic  2.15 us (3%)
  between operations  0.64 us (1%)
    pallas_call x1, Pallas kernels, shards(): pl.pallas_call(kernel, out_shape=(jax.ShapeDtypeStruct((rows, width), BF1...  59.9 us
    add x1, other arithmetic, shards(): return (sources, transported + 0.5 * sources)  2.15 us

profile of v4, /device:TPU:1, one launch (start us, length us, event | category | flops | bytes accessed | tf_op | source)
XLA Modules:
  0.0 62.7 jit_solution(1877460518823103894)
XLA Ops:
  0.6 59.9 %shard_map.95 = (bf16[512,256]{1,0:T(8,128)(2,1)}, f32[512,256]{1,0:T(8,128)}) custom-call(s32[4,128]{1,0:T(4,128)} %bitcast.1, bf16[512]{0:T(512)(128)(2,1)} %off_in.1, f32[8193]{0:T(1024)} %speeds_in.1, f32[512,256]{1,0:T(8,128)} %pop.1, bf16[1,256,4096]{2,1,0:T(8,128)(2,1)} %rate.1, bf16[1,256,4096]{2,1,0:T(8,128)(2,1)} %slope.1, f32[1,256]{1,0:T(1,128)} %rate_gain_in.1, ...), custom_call_target="tpu_custom_call" | custom-call | tf_op jit(solution)/shard_map/pallas_call | solution.py:575
  60.5 2.2 %multiply_add_fusion = (f32[512,256]{1,0:T(8,128)}, f32[512,256]{1,0:T(8,128)}) fusion(f32[512,256]{1,0:T(8,128)} %get-tuple-element.5, bf16[512,256]{1,0:T(8,128)(2,1)} %get-tuple-element.4), kind=kLoop, calls=%fused_computation | loop fusion | flops 393216 | bytes 1835008 | tf_op jit(solution)/shard_map/add | solution.py:621

commit v5 on v4

--- a/solution.py
+++ b/solution.py
@@ -374,22 +374,23 @@
         enter(1)
         turn(0, 2, {})
         wait_weights()
-        turn(1, 1, {3: own(0, 0, True)})
-        turn(0, 3, {1: own(0, -1), 3: own(0, 1)})
+        turn(1, 1, {0: own(0, 0, True), 2: other(0, 0)})
+        turn(0, 3, {0: other(0, 1), 2: other(0, 2)})
         send_offsets()
-        turn(1, 2, {1: other(0, 0)})
+        turn(1, 2, {1: own(0, -1), 3: own(0, 1)})
         enter(2)
         enter(3)
-        leave(0, {})
-        turn(1, 3, {1: other(0, 1), 3: other(0, 2)})
-        turn(2, 1, {1: own(0, -2), 3: own(0, 2)})
-        turn(3, 1, {0: other(0, 3), 2: other(0, 4)})
-        leave(1, {0: own(0, -3), 2: own(0, 3)})
-        turn(2, 2, {0: other(0, 5), 1: own(0, HOPS), 3: other(0, 6)})
-        turn(3, 2, {0: own(1, 0, True), 1: own(1, -1), 2: own(1, 1), 3: other(1, 0)})
+        leave(0, {1: own(0, -2), 3: own(0, 2)})
+        turn(1, 3, {1: other(0, 3), 3: other(0, 4)})
+        turn(2, 1, {1: own(0, -3), 3: own(0, 3)})
+        turn(3, 1, {1: other(0, 5)})
+        leave(1, {})
+        turn(2, 2, {0: own(0, HOPS), 2: own(1, 0, True)})
+        turn(3, 2, {0: own(1, -1), 2: own(1, 1), 3: other(1, 0)})
         turn(2, 3, {0: other(1, 1), 2: other(1, 2)})
-        turn(3, 3, {0: other(0, 7), 1: lambda: finish(0, 0, batch), 2: own(1, -2), 3: own(1, 2)})
-        leave(2, {0: other(1, 3), 2: other(1, 4)})
+        turn(3, 3, {0: other(0, 6), 1: other(0, 7), 2: lambda: finish(0, 0, batch), 3: own(1, -2)})
+        leave(2, {0: own(1, 2), 1: other(1, 3), 2: other(1, 4)})
+
         def half_own(s):
             multiply(1, 0, -3, s * near, near)
             multiply(1, 0, 3, s * near, near)
@@ -499,21 +500,22 @@
         multiply_two(0, 0, 1)
         pass_on(1, 7)
         arrived(0, 5)
-        arrived(0, 6)
         arrived(1, 0)
-        multiply_two(0, 1, 3)
+        multiply(0, 1, -3)
         wait_padded(2, 2, 0, batch)
         multiply_two(0, 0, 2)
         arrived(1, 1)
         arrived(1, 2)
         wait_padded(3, 2, 0, batch)
         multiply_two(0, 0, 3)
+        multiply(1, 1, 0, fresh=True)
+        arrived(0, 6)
+        multiply(0, 1, 3)
         arrived(0, 7)
         multiply(0, 1, HOPS)
         wait_padded(HOPS, 1, 0, batch)
         multiply(0, 0, HOPS)
         finish(0, 0, batch)
-        multiply(1, 1, 0, fresh=True)
         wait_padded(5, 1, batch, batch)
         multiply(1, 0, 0)
         arrived(1, 3)

time: 62.8 us -> 62.7 us (level)
  no operation moved by 1% of the time
where the time goes in v5:
time: 62.7 us; the launch traced here: 62.6 us
  Pallas kernels  59.8 us (95%)
  other arithmetic  2.15 us (3%)
  between operations  0.64 us (1%)
    pallas_call x1, Pallas kernels, shards(): pl.pallas_call(kernel, out_shape=(jax.ShapeDtypeStruct((rows, width), BF1...  59.8 us
    add x1, other arithmetic, shards(): return (sources, transported + 0.5 * sources)  2.15 us

profile of v5, /device:TPU:1, one launch (start us, length us, event | category | flops | bytes accessed | tf_op | source)
XLA Modules:
  0.0 62.6 jit_solution(1191113803161227638)
XLA Ops:
  0.6 59.8 %shard_map.95 = (bf16[512,256]{1,0:T(8,128)(2,1)}, f32[512,256]{1,0:T(8,128)}) custom-call(s32[4,128]{1,0:T(4,128)} %bitcast.1, bf16[512]{0:T(512)(128)(2,1)} %off_in.1, f32[8193]{0:T(1024)} %speeds_in.1, f32[512,256]{1,0:T(8,128)} %pop.1, bf16[1,256,4096]{2,1,0:T(8,128)(2,1)} %rate.1, bf16[1,256,4096]{2,1,0:T(8,128)(2,1)} %slope.1, f32[1,256]{1,0:T(1,128)} %rate_gain_in.1, ...), custom_call_target="tpu_custom_call" | custom-call | tf_op jit(solution)/shard_map/pallas_call | solution.py:577
  60.5 2.2 %multiply_add_fusion = (f32[512,256]{1,0:T(8,128)}, f32[512,256]{1,0:T(8,128)}) fusion(f32[512,256]{1,0:T(8,128)} %get-tuple-element.5, bf16[512,256]{1,0:T(8,128)(2,1)} %get-tuple-element.4), kind=kLoop, calls=%fused_computation | loop fusion | flops 393216 | bytes 1835008 | tf_op jit(solution)/shard_map/add | solution.py:623
